TPU v7x, 32 devices: a whole 2x2x4 slice. The times are simulated.
32 devices in a mesh: lines: 2 (over y), shots: 16 (over z, x, core).
Axes of the slice: x: 2, y: 2, z: 4, core: 2. Of those that a mesh axis runs over, the one named last changes fastest.
Arguments:
- records: bfloat16 [2048, 1024, 256], P(('lines', 'shots')), parts along dimension 0, may hold values from -6 to 6
- missing: int32 [256], P('lines'), parts along dimension 0, may hold values from 0 to 1023, as said below
- neighbours: int32 [256, 3], P('lines'), parts along dimension 0, may hold values from 0 to 1023, as said below
- weights: float32 [256, 3], P('lines'), parts along dimension 0, may hold values from 0.2 to 0.6
- freq_bins: int32 [8], replicated, may hold values from 1 to 127, as said below
Outputs:
- multiples: bfloat16 [2048, 1024, 256], P(('lines', 'shots')), parts along dimension 0
There are 2 independent parts, one for each index of `lines`. A program takes and returns all parts, laid end to end along the dimension named above; an argument that names none is the same for every part. Nothing has to cross between parts.
Inputs may be any that keep to these rules, and one draw needn't show every extreme that they name: `missing`: distinct and ascending; any two missing shots lie 3 or more apart, and every shot within 2 of a missing shot is recorded. `neighbours`: row i names 3 distinct recorded shots, each within 2 of missing[i]. `freq_bins`: 8 distinct bins.
All inputs are finite; a program needn't handle non-finite values.
Results may differ from a plain program's by a relative error of at most 0.0079.
Values may be sent and summed in bfloat16 or wider, within the bound.
No kernel may reach another device: no remote copies, remote signals or barrier semaphores. Data moves between devices by JAX's collectives and lax.ppermute only.
A program may use at most 192 MiB of HBM per device.

v0:
```python
import math
import jax
import jax.numpy as jnp
from jax import lax
from jax.sharding import PartitionSpec as P


def from_partner(array, axis, stride):
    return lax.ppermute(array, axis, [(i, i ^ 1 << stride) for i in range(lax.axis_size(axis))])


def tables(freq_bins, sample_count):
    bin_count = freq_bins.shape[0]
    sample_ids = jnp.arange(sample_count, dtype=jnp.int32)
    phases = freq_bins[None, :] * sample_ids[:, None] % sample_count
    angles = phases.astype(jnp.float32) * (2.0 * math.pi / sample_count)
    trig_pair = jnp.stack([jnp.cos(angles), -jnp.sin(angles)], axis=-1)
    forward = (trig_pair / math.sqrt(sample_count)).astype(jnp.bfloat16)
    inverse = (trig_pair * math.sqrt(2.0 / bin_count)).astype(jnp.bfloat16)
    return (forward, inverse)


def add_block(summed, right_source, block_piece, source_part, width):
    right_rows = lax.dynamic_slice_in_dim(right_source, source_part * width, width, 2)
    right_real = right_rows[:, 0]
    right_imag = right_rows[:, 1]
    left_side = jnp.concatenate([block_piece[:, 0], block_piece[:, 1]], axis=-1)
    right_side = jnp.concatenate(
        [
            jnp.concatenate([right_real, right_imag], axis=-1),
            jnp.concatenate([-right_imag, right_real], axis=-1),
        ],
        axis=1,
    )
    return summed + jnp.einsum(
        "zsk,zkc->zsc", left_side, right_side, preferred_element_type=jnp.float32
    )


def shards(records, missing, neighbours, weights, freq_bins):
    devices = lax.axis_size("shots")
    position = lax.axis_index("shots")
    shot_rows = records.shape[0]
    matrix_order = records.shape[1]
    sample_count = records.shape[2]
    half = matrix_order // 2
    couples = devices // 2
    neigh_count = neighbours.shape[1]
    forward, inverse = tables(freq_bins, sample_count)
    blocked = records.reshape(shot_rows, 2, half, sample_count)
    spectra = jnp.einsum(
        "shrt,tpc->phcsr", blocked, forward, preferred_element_type=jnp.float32
    ).astype(jnp.bfloat16)
    outgoing = spectra.reshape(devices, 2, shot_rows, half)
    incoming = lax.all_to_all(outgoing, "shots", split_axis=0, concat_axis=2, tiled=True)
    own_block = incoming
    filled_rows = jnp.zeros(
        own_block.shape[:2] + (missing.shape[0], own_block.shape[3]), jnp.float32
    )
    for slot_index in range(neigh_count):
        picked = jnp.take(own_block, neighbours[:, slot_index], axis=2)
        filled_rows = filled_rows + weights[:, slot_index][:, None] * picked.astype(jnp.float32)
    own_block = own_block.at[:, :, missing, :].set(filled_rows.astype(jnp.bfloat16))
    factor = -1.0 / math.sqrt(matrix_order)
    member = position % 2
    other_half = from_partner(own_block, "shots", 0)
    summed = jnp.zeros((1, matrix_order, 2 * half), jnp.float32)
    summed = add_block(summed, own_block, own_block, member, half)
    summed = add_block(summed, own_block, other_half, 1 - member, half)
    predicted = (summed * factor).astype(jnp.bfloat16)
    outgoing_back = predicted.reshape(1, 1, matrix_order, 2, half)
    returned = lax.all_to_all(outgoing_back, "shots", split_axis=2, concat_axis=0, tiled=True)
    returned = returned.reshape(couples, 2, shot_rows, 2, half)
    inverse_pair = jnp.transpose(inverse, (1, 2, 0))
    multiples = jnp.einsum(
        "phsir,pit->shrt", returned, inverse_pair, preferred_element_type=jnp.float32
    )
    return multiples.astype(jnp.bfloat16).reshape(shot_rows, matrix_order, sample_count)


def solution(mesh):
    return jax.shard_map(
        shards,
        mesh=mesh,
        in_specs=(
            P(("lines", "shots"), None, None),
            P("lines"),
            P("lines", None),
            P("lines", None),
            P(),
        ),
        out_specs=P(("lines", "shots"), None, None),
        check_vma=False,
    )
```

profile of v0, /device:TPU:1, one launch (start us, length us, event | category | flops | bytes accessed | tf_op | source)
XLA Modules:
  0.0 226.2 jit_solution(15952306101126947677)
XLA Ops:
  0.0 0.8 fusion.33
  0.8 14.2 %convert_bitcast_fusion = bf16[8,2,2,64,512]{4,0,1,3,2:T(8,128)(2,1)S(1)} fusion(bf16[64,2,512,256,1]{3,2,1,0,4:T(8,128)(2,1)} %bitcast.127, f32[256,8,1]{0,1,2:T(8,128)S(1)} %get-tuple-element.30, f32[256,8,1]{0,1,2:T(8,128)S(1)} %get-tuple-element.29), kind=kOutput, calls=%fused_computation.31 | convolution fusion | flops 537931776 | bytes 35667968 | tf_op jit(solution)/shard_map/shrt,tpc->phcsr/dot_general | solution.py:51
  15.0 2.5 %copy.40 = bf16[8,2,2,64,512]{4,3,2,1,0:T(8,128)(2,1)} copy(bf16[8,2,2,64,512]{4,0,1,3,2:T(8,128)(2,1)S(1)} %convert_bitcast_fusion) | data formatting | bytes 4194304 | tf_op jit(solution)/shard_map/convert_element_type | solution.py:53
  17.5 7.4 %all-to-all-start = ((bf16[16,2,64,512]{3,2,1,0:T(8,128)(2,1)}), bf16[16,2,64,512]{3,2,1,0:T(8,128)(2,1)S(1)}, u32[]{:S(2)}, u32[]{:S(2)}) async-start(bf16[16,2,64,512]{3,2,1,0:T(8,128)(2,1)} %bitcast.131), calls=%async_computation | async-start | bytes 4194304 | tf_op jit(solution)/shard_map/all_to_all | solution.py:55
  25.0 41.4 %all-to-all-done = bf16[16,2,64,512]{3,2,1,0:T(8,128)(2,1)S(1)} async-done(((bf16[16,2,64,512]{3,2,1,0:T(8,128)(2,1)}), bf16[16,2,64,512]{3,2,1,0:T(8,128)(2,1)S(1)}, u32[]{:S(2)}, u32[]{:S(2)}) %all-to-all-start) | async-done | bytes 2097184 | tf_op jit(solution)/shard_map/all_to_all | solution.py:55
  66.4 1.3 copy-done
  67.8 3.9 %copy.41 = bf16[1,2,16,64,512]{4,1,3,2,0:T(2,128)(2,1)S(1)} copy(bf16[1,2,16,64,512]{4,3,1,2,0:T(8,128)(2,1)} %bitcast.128) | data formatting | bytes 4194304 | tf_op jit(solution)/shard_map/all_to_all | solution.py:55
  71.7 0.2 copy.42
  71.9 3.5 %copy.77 = bf16[1,2,1024,512]{3,1,2,0:T(2,128)(2,1)} copy(bf16[1,2,1024,512]{3,2,1,0:T(8,128)(2,1)S(1)} %bitcast.132) | data formatting | bytes 4194304 | tf_op jit(solution)/shard_map/all_to_all | solution.py:55
  75.4 2.7 %gather_fusion.2 = bf16[128,2,512]{2,1,0:T(2,128)(2,1)S(1)} fusion(bf16[2,1024,512]{2,0,1:T(2,128)(2,1)} %bitcast.137, s32[1024]{0:T(1024)S(1)} %get-tuple-element.31), kind=kCustom, calls=%fused_computation.2.clone | custom fusion | bytes 524800 | tf_op jit(solution)/shard_map/jit(_take)/gather | solution.py:61
  78.1 2.7 %gather_fusion.1 = bf16[128,2,512]{2,1,0:T(2,128)(2,1)S(1)} fusion(bf16[2,1024,512]{2,0,1:T(2,128)(2,1)} %bitcast.138, s32[1024]{0:T(1024)S(1)} %get-tuple-element.32), kind=kCustom, calls=%fused_computation.1.clone | custom fusion | bytes 524800 | tf_op jit(solution)/shard_map/jit(_take)/gather | solution.py:61
  80.8 2.7 %gather_fusion = bf16[128,2,512]{2,1,0:T(2,128)(2,1)S(1)} fusion(bf16[2,1024,512]{2,0,1:T(2,128)(2,1)} %bitcast.139, s32[1024]{0:T(1024)S(1)} %pad_clamp_fusion.2), kind=kCustom, calls=%fused_computation.clone | custom fusion | bytes 524800 | tf_op jit(solution)/shard_map/jit(_take)/gather | solution.py:61
  83.6 0.3 fusion.20
  83.9 0.3 copy.49
  84.1 4.4 %scatter_fusion = bf16[2,1024,512]{2,0,1:T(2,128)(2,1)S(1)} fusion(bf16[2,1024,512]{2,0,1:T(2,128)(2,1)S(1)} %bitcast.124, s32[128]{0:T(128)S(1)} %compare_select_fusion.3, bf16[128,2,512]{2,1,0:T(2,128)(2,1)S(1)} %copy.49), kind=kCustom, calls=%fused_computation.3 | custom fusion | bytes 786944 | tf_op jit(solution)/shard_map/scatter | solution.py:63
  88.5 1.4 constant_dynamic-slice_fusion
  90.0 0.2 copy.82
  90.2 0.2 copy.83
  90.3 0.1 collective-permute-start
  90.4 3.2 %fusion.43 = (bf16[1,1,1024,512]{3,1,2,0:T(2,128)(2,1)S(1)}, bf16[1,1,1024,512]{3,1,2,0:T(2,128)(2,1)S(1)}) fusion(bf16[1,2,1024,512]{3,1,2,0:T(2,128)(2,1)S(1)} %bitcast.126), kind=kLoop, calls=%fused_computation.89 | loop fusion | bytes 4194304 | tf_op jit(solution)/shard_map/slice | solution.py:27
  93.6 0.3 copy.81
  93.9 0.3 copy.80
  94.3 0.1 slice_bitcast_fusion
  94.5 2.5 %fusion.1 = f32[1024,1024]{0,1:T(8,128)S(1)} fusion(bf16[1,1024,512]{2,1,0:T(8,128)(2,1)S(1)} %bitcast.142, bf16[1,1024,512]{2,1,0:T(8,128)(2,1)S(1)} %bitcast.141, bf16[1,512,512]{2,1,0:T(8,128)(2,1)S(1)} %get-tuple-element.21, bf16[1,512,512]{2,1,0:T(8,128)(2,1)S(1)} %fusion.40, bf16[1,512,512]{2,1,0:T(8,128)(2,1)S(1)} %get-tuple-element.20), kind=kOutput, calls=%fused_computation.8 | convolution fusion | flops 2160066560 | bytes 7864320 | tf_op jit(solution)/shard_map/zsk,zkc->zsc/dot_general | solution.py:35
  96.9 3.0 %fusion.42 = (bf16[1,1,1024,512]{3,1,2,0:T(2,128)(2,1)S(1)}, bf16[1,1,1024,512]{3,1,2,0:T(2,128)(2,1)S(1)}) fusion(bf16[1,2,1024,512]{3,1,2,0:T(2,128)(2,1)S(1)} %collective-permute-done), kind=kLoop, calls=%fused_computation.88 | loop fusion | bytes 4194304 | tf_op jit(solution)/shard_map/slice | solution.py:27
  99.9 0.3 copy.79
  100.2 0.3 copy.78
  100.5 4.0 %multiply_convert_fusion = bf16[1024,1024]{0,1:T(8,128)(2,1)} fusion(f32[1024,1024]{0,1:T(8,128)S(1)} %fusion.1, bf16[1,512,512]{2,1,0:T(8,128)(2,1)S(1)} %get-tuple-element.19, bf16[1,512,512]{2,1,0:T(8,128)(2,1)S(1)} %fusion.41, bf16[1,512,512]{2,1,0:T(8,128)(2,1)S(1)} %get-tuple-element.18, bf16[1,1024,512]{2,1,0:T(8,128)(2,1)S(1)} %bitcast.144, ...), kind=kOutput, calls=%fused_computation.6 | convolution fusion | flops 2163212288 | bytes 9961472 | tf_op jit(solution)/shard_map/zsk,zkc->zsc/dot_general | solution.py:35
  104.5 4.8 %copy.52 = bf16[1,1,1024,2,512]{4,3,1,0,2:T(2,128)(2,1)S(1)} copy(bf16[1,1,1024,2,512]{2,4,3,1,0:T(8,128)(2,1)} %bitcast.140) | data formatting | bytes 4194304 | tf_op jit(solution)/shard_map/reshape | solution.py:71
  109.3 58.5 %all_to_all.27 = bf16[1,1,1024,2,512]{4,3,1,0,2:T(2,128)(2,1)S(1)} all-to-all(bf16[1,1,1024,2,512]{4,3,1,0,2:T(2,128)(2,1)S(1)} %copy.52), channel_id=1, replica_groups=mesh['lines'=2,'shots'=16] {'shots'}, dimensions={2} | all-to-all | bytes 4194304 | tf_op jit(solution)/shard_map/all_to_all | solution.py:72
  167.8 14.1 %fusion = bf16[64,2,512,256]{2,3,0,1:T(8,128)(2,1)} fusion(bf16[8,2,64,2,512]{4,3,2,1,0:T(2,128)(2,1)S(1)} %bitcast.130, f32[256,8,1]{0,1,2:T(8,128)S(1)} %get-tuple-element.30, f32[256,8,1]{0,1,2:T(8,128)S(1)} %get-tuple-element.29), kind=kOutput, calls=%fused_computation.5 | convolution fusion | flops 553660416 | bytes 35667968 | tf_op jit(solution)/shard_map/phsir,pit->shrt/dot_general | solution.py:75
  181.9 44.2 %copy.55 = bf16[64,2,512,256]{3,2,1,0:T(8,128)(2,1)} copy(bf16[64,2,512,256]{2,3,0,1:T(8,128)(2,1)} %fusion) | data formatting | bytes 67108864 | tf_op jit(solution)/shard_map/convert_element_type | solution.py:78
  (18 shorter events, 0.2 us)
Async XLA Ops:
  17.5 7.5 %copy-start.3 = (s32[128,3]{0,1:T(4,128)S(1)}, s32[128,3]{0,1:T(4,128)}, u32[]{:S(2)}) copy-start(s32[128,3]{0,1:T(4,128)} %param.9) | copy-start | bytes 4612
  17.5 7.5 %copy-start.4 = (s32[128]{0:T(128)S(1)}, s32[128]{0:T(128)}, u32[]{:S(2)}) copy-start(s32[128]{0:T(128)} %param.8) | copy-start | bytes 1540
  17.5 7.5 %copy-start.2 = (f32[128,3]{0,1:T(4,128)S(1)}, f32[128,3]{0,1:T(4,128)}, u32[]{:S(2)}) copy-start(f32[128,3]{0,1:T(4,128)} %param.10) | copy-start | bytes 4612
  17.5 49.0 %all-to-all-start = ((bf16[16,2,64,512]{3,2,1,0:T(8,128)(2,1)}), bf16[16,2,64,512]{3,2,1,0:T(8,128)(2,1)S(1)}, u32[]{:S(2)}, u32[]{:S(2)}) async-start(bf16[16,2,64,512]{3,2,1,0:T(8,128)(2,1)} %bitcast.131), calls=%async_computation | async-start | bytes 4194304 | tf_op jit(solution)/shard_map/all_to_all | solution.py:55
  66.4 1.3 copy-start
  67.8 3.9 %copy-start.1 = (bf16[16,2,64,512]{3,2,1,0:T(8,128)(2,1)S(1)}, bf16[16,2,64,512]{3,2,1,0:T(8,128)(2,1)}, u32[]{:S(2)}) copy-start(bf16[16,2,64,512]{3,2,1,0:T(8,128)(2,1)} %copy-done) | copy-start | bytes 6291460
  90.3 6.6 %collective-permute-start = (bf16[1,2,1024,512]{3,1,2,0:T(2,128)(2,1)S(1)}, bf16[1,2,1024,512]{3,1,2,0:T(2,128)(2,1)S(1)}, u32[]{:S(2)}, u32[]{:S(2)}) collective-permute-start(bf16[1,2,1024,512]{3,1,2,0:T(2,128)(2,1)S(1)} %bitcast.125), channel_id=1, source_target_pairs={{0,1},{1,0},{2,3},{3,2},{4,5},{5,4},{6,7},{7,6},{8,9},{9,8},{10,11... | collective-permute-start | bytes 6291464 | tf_op jit(solution)/shard_map/ppermute | solution.py:9
where the time goes:
time: 228 us; the launch traced here: 226 us
  local copies, waits for them, and re-layouts  82.5 us (36%)
  blocking collectives  58.5 us (26%)
  waiting for transfers between devices  41.4 us (18%)
  matrix products  34.7 us (15%)
  starting transfers between devices  7.51 us (3%)
    all_to_all x1, blocking collectives, shards(): lax.all_to_all(outgoing_back, 'shots', split_axis=2, concat_axis=0, tiled...  58.5 us
    convert_element_type x1, local copies, waits for them, and re-layouts, shards(): multiples.astype(jnp.bfloat16)  44.2 us
    all_to_all x1, waiting for transfers between devices, shards(): lax.all_to_all(outgoing, 'shots', split_axis=0, concat_axis=2, tiled=True)  41.4 us
    dot_general x1, matrix products, shards(): jnp.einsum('shrt,tpc->phcsr', blocked, forward, preferred_element_type=jn...  14.2 us
    dot_general x1, matrix products, shards(): jnp.einsum('phsir,pit->shrt', returned, inverse_pair, preferred_element_t...  14.1 us
    gather x3, local copies, waits for them, and re-layouts, shards(): picked = jnp.take(own_block, neighbours[:, slot_index], axis=2)  8.18 us
    all_to_all x3, local copies, waits for them, and re-layouts, shards(): lax.all_to_all(outgoing, 'shots', split_axis=0, concat_axis=2, tiled=True)  7.59 us
    all_to_all x1, starting transfers between devices, shards(): lax.all_to_all(outgoing, 'shots', split_axis=0, concat_axis=2, tiled=True)  7.44 us
  transfers between devices with their start and end apart: 2, of which 1 were waited for; matrix products, arithmetic and copies ran while one was open for 3% of the time, Pallas kernels for 0%

commit v1 on v0

--- a/solution.py
+++ b/solution.py
@@ -52,7 +52,12 @@
         "shrt,tpc->phcsr", blocked, forward, preferred_element_type=jnp.float32
     ).astype(jnp.bfloat16)
     outgoing = spectra.reshape(devices, 2, shot_rows, half)
-    incoming = lax.all_to_all(outgoing, "shots", split_axis=0, concat_axis=2, tiled=True)
+    incoming = jnp.concatenate(
+        lax.all_to_all(
+            jnp.stack(jnp.split(outgoing, lax.axis_size("shots"), axis=0)), "shots", 0, 0
+        ),
+        axis=2,
+    )
     own_block = incoming
     filled_rows = jnp.zeros(
         own_block.shape[:2] + (missing.shape[0], own_block.shape[3]), jnp.float32

time: 228 us -> 237 us (1.039)
  local copies, waits for them, and re-layouts: 82.5 us -> 91.8 us
    unnamed x17 -> x32, local copies, waits for them, and re-layouts: 4.25 us -> 14.2 us
    all_to_all x3 -> x0, local copies, waits for them, and re-layouts: 7.59 us -> none  [shards(): lax.all_to_all(outgoing, 'shots', split_axis=0, concat_axis=2, tiled=True)]
    reshape x0 -> x3, local copies, waits for them, and re-layouts: none -> 7.59 us  [shards(): jnp.concatenate(lax.all_to_all(jnp.stack(jnp.split(outgoing, lax.axis_siz...]
where the time goes in v1:
time: 237 us; the launch traced here: 235 us
  local copies, waits for them, and re-layouts  91.8 us (39%)
  blocking collectives  58.5 us (25%)
  waiting for transfers between devices  41.4 us (17%)
  matrix products  34.7 us (15%)
  starting transfers between devices  7.51 us (3%)
    all_to_all x1, blocking collectives, shards(): lax.all_to_all(outgoing_back, 'shots', split_axis=2, concat_axis=0, tiled...  58.5 us
    convert_element_type x1, local copies, waits for them, and re-layouts, shards(): multiples.astype(jnp.bfloat16)  44.2 us
    all_to_all x1, waiting for transfers between devices, shards(): lax.all_to_all(jnp.stack(jnp.split(outgoing, lax.axis_size('shots'), axis...  41.4 us
    unnamed x32, local copies, waits for them, and re-layouts  14.2 us
    dot_general x1, matrix products, shards(): jnp.einsum('shrt,tpc->phcsr', blocked, forward, preferred_element_type=jn...  14.2 us
    dot_general x1, matrix products, shards(): jnp.einsum('phsir,pit->shrt', returned, inverse_pair, preferred_element_t...  14.1 us
    gather x3, local copies, waits for them, and re-layouts, shards(): picked = jnp.take(own_block, neighbours[:, slot_index], axis=2)  8.18 us
    reshape x3, local copies, waits for them, and re-layouts, shards(): jnp.concatenate(lax.all_to_all(jnp.stack(jnp.split(outgoing, lax.axis_siz...  7.59 us
  transfers between devices with their start and end apart: 2, of which 1 were waited for; matrix products, arithmetic and copies ran while one was open for 3% of the time, Pallas kernels for 0%

profile of v1, /device:TPU:1, one launch (start us, length us, event | category | flops | bytes accessed | tf_op | source)
XLA Modules:
  0.0 235.5 jit_solution(17644771592506310387)
XLA Ops:
  0.0 0.8 fusion.49
  0.8 14.2 %convert_bitcast_fusion = bf16[8,2,2,64,512]{4,0,1,3,2:T(8,128)(2,1)S(1)} fusion(bf16[64,2,512,256,1]{3,2,1,0,4:T(8,128)(2,1)} %bitcast.189, f32[256,8,1]{0,1,2:T(8,128)S(1)} %get-tuple-element.30, f32[256,8,1]{0,1,2:T(8,128)S(1)} %get-tuple-element.29), kind=kOutput, calls=%fused_computation.31 | convolution fusion | flops 537931776 | bytes 35667968 | tf_op jit(solution)/shard_map/shrt,tpc->phcsr/dot_general | solution.py:51
  15.0 1.2 copy.55
  16.1 0.7 fusion.36
  16.8 0.7 fusion.35
  17.5 0.7 fusion.34
  18.1 0.7 fusion.33
  18.8 0.7 fusion.32
  19.5 0.7 fusion.31
  20.1 0.7 fusion.30
  20.8 0.7 fusion.29
  21.5 0.7 fusion.28
  22.1 0.7 fusion.27
  22.8 0.7 fusion.26
  26.8 7.4 %all-to-all-start = ((bf16[16,1,2,64,512]{4,3,2,1,0:T(8,128)(2,1)}), bf16[16,1,2,64,512]{4,3,2,1,0:T(8,128)(2,1)S(1)}, u32[]{:S(2)}, u32[]{:S(2)}) async-start(bf16[16,1,2,64,512]{4,3,2,1,0:T(8,128)(2,1)} %fusion.21), calls=%async_computation | async-start | bytes 4194304 | tf_op jit(solution)/shard_map/all_to_all | solution.py:56
  34.3 41.4 %all-to-all-done = bf16[16,1,2,64,512]{4,3,2,1,0:T(8,128)(2,1)S(1)} async-done(((bf16[16,1,2,64,512]{4,3,2,1,0:T(8,128)(2,1)}), bf16[16,1,2,64,512]{4,3,2,1,0:T(8,128)(2,1)S(1)}, u32[]{:S(2)}, u32[]{:S(2)}) %all-to-all-start) | async-done | bytes 2097184 | tf_op jit(solution)/shard_map/all_to_all | solution.py:56
  75.8 1.3 copy-done
  77.1 3.9 %copy.56 = bf16[1,2,16,64,512]{4,1,3,2,0:T(2,128)(2,1)S(1)} copy(bf16[1,2,16,64,512]{4,3,1,0,2:T(8,128)(2,1)} %bitcast.190) | data formatting | bytes 4194304 | tf_op jit(solution)/shard_map/reshape | solution.py:55
  81.2 3.5 %copy.92 = bf16[1,2,1024,512]{3,1,2,0:T(2,128)(2,1)} copy(bf16[1,2,1024,512]{3,2,1,0:T(8,128)(2,1)S(1)} %bitcast.209) | data formatting | bytes 4194304 | tf_op jit(solution)/shard_map/reshape | solution.py:55
  84.7 2.7 %gather_fusion.2 = bf16[128,2,512]{2,1,0:T(2,128)(2,1)S(1)} fusion(bf16[2,1024,512]{2,0,1:T(2,128)(2,1)} %bitcast.214, s32[1024]{0:T(1024)S(1)} %get-tuple-element.31), kind=kCustom, calls=%fused_computation.2.clone | custom fusion | bytes 524800 | tf_op jit(solution)/shard_map/jit(_take)/gather | solution.py:66
  87.4 2.7 %gather_fusion.1 = bf16[128,2,512]{2,1,0:T(2,128)(2,1)S(1)} fusion(bf16[2,1024,512]{2,0,1:T(2,128)(2,1)} %bitcast.215, s32[1024]{0:T(1024)S(1)} %get-tuple-element.32), kind=kCustom, calls=%fused_computation.1.clone | custom fusion | bytes 524800 | tf_op jit(solution)/shard_map/jit(_take)/gather | solution.py:66
  90.2 2.7 %gather_fusion = bf16[128,2,512]{2,1,0:T(2,128)(2,1)S(1)} fusion(bf16[2,1024,512]{2,0,1:T(2,128)(2,1)} %bitcast.216, s32[1024]{0:T(1024)S(1)} %pad_clamp_fusion.2), kind=kCustom, calls=%fused_computation.clone | custom fusion | bytes 524800 | tf_op jit(solution)/shard_map/jit(_take)/gather | solution.py:66
  93.5 4.4 %scatter_fusion = bf16[2,1024,512]{2,0,1:T(2,128)(2,1)S(1)} fusion(bf16[2,1024,512]{2,0,1:T(2,128)(2,1)S(1)} %bitcast.186, s32[128]{0:T(128)S(1)} %compare_select_fusion.3, bf16[128,2,512]{2,1,0:T(2,128)(2,1)S(1)} %copy.64), kind=kCustom, calls=%fused_computation.3 | custom fusion | bytes 786944 | tf_op jit(solution)/shard_map/scatter | solution.py:68
  97.8 1.4 constant_dynamic-slice_fusion
  99.7 3.2 %fusion.59 = (bf16[1,1,1024,512]{3,1,2,0:T(2,128)(2,1)S(1)}, bf16[1,1,1024,512]{3,1,2,0:T(2,128)(2,1)S(1)}) fusion(bf16[1,2,1024,512]{3,1,2,0:T(2,128)(2,1)S(1)} %bitcast.188), kind=kLoop, calls=%fused_computation.121 | loop fusion | bytes 4194304 | tf_op jit(solution)/shard_map/slice | solution.py:27
  103.8 2.5 %fusion.1 = f32[1024,1024]{0,1:T(8,128)S(1)} fusion(bf16[1,1024,512]{2,1,0:T(8,128)(2,1)S(1)} %bitcast.219, bf16[1,1024,512]{2,1,0:T(8,128)(2,1)S(1)} %bitcast.218, bf16[1,512,512]{2,1,0:T(8,128)(2,1)S(1)} %get-tuple-element.21, bf16[1,512,512]{2,1,0:T(8,128)(2,1)S(1)} %fusion.56, bf16[1,512,512]{2,1,0:T(8,128)(2,1)S(1)} %get-tuple-element.20), kind=kOutput, calls=%fused_computation.8 | convolution fusion | flops 2160066560 | bytes 7864320 | tf_op jit(solution)/shard_map/zsk,zkc->zsc/dot_general | solution.py:35
  106.2 3.0 %fusion.58 = (bf16[1,1,1024,512]{3,1,2,0:T(2,128)(2,1)S(1)}, bf16[1,1,1024,512]{3,1,2,0:T(2,128)(2,1)S(1)}) fusion(bf16[1,2,1024,512]{3,1,2,0:T(2,128)(2,1)S(1)} %collective-permute-done), kind=kLoop, calls=%fused_computation.120 | loop fusion | bytes 4194304 | tf_op jit(solution)/shard_map/slice | solution.py:27
  109.8 4.0 %multiply_convert_fusion = bf16[1024,1024]{0,1:T(8,128)(2,1)} fusion(f32[1024,1024]{0,1:T(8,128)S(1)} %fusion.1, bf16[1,512,512]{2,1,0:T(8,128)(2,1)S(1)} %get-tuple-element.19, bf16[1,512,512]{2,1,0:T(8,128)(2,1)S(1)} %fusion.57, bf16[1,512,512]{2,1,0:T(8,128)(2,1)S(1)} %get-tuple-element.18, bf16[1,1024,512]{2,1,0:T(8,128)(2,1)S(1)} %bitcast.221, ...), kind=kOutput, calls=%fused_computation.6 | convolution fusion | flops 2163212288 | bytes 9961472 | tf_op jit(solution)/shard_map/zsk,zkc->zsc/dot_general | solution.py:35
  113.8 4.8 %copy.67 = bf16[1,1,1024,2,512]{4,3,1,0,2:T(2,128)(2,1)S(1)} copy(bf16[1,1,1024,2,512]{2,4,3,1,0:T(8,128)(2,1)} %bitcast.217) | data formatting | bytes 4194304 | tf_op jit(solution)/shard_map/reshape | solution.py:76
  118.6 58.5 %all_to_all.14 = bf16[1,1,1024,2,512]{4,3,1,0,2:T(2,128)(2,1)S(1)} all-to-all(bf16[1,1,1024,2,512]{4,3,1,0,2:T(2,128)(2,1)S(1)} %copy.67), channel_id=1, replica_groups=mesh['lines'=2,'shots'=16] {'shots'}, dimensions={2} | all-to-all | bytes 4194304 | tf_op jit(solution)/shard_map/all_to_all | solution.py:77
  177.1 14.1 %fusion = bf16[64,2,512,256]{2,3,0,1:T(8,128)(2,1)} fusion(bf16[8,2,64,2,512]{4,3,2,1,0:T(2,128)(2,1)S(1)} %bitcast.192, f32[256,8,1]{0,1,2:T(8,128)S(1)} %get-tuple-element.30, f32[256,8,1]{0,1,2:T(8,128)S(1)} %get-tuple-element.29), kind=kOutput, calls=%fused_computation.5 | convolution fusion | flops 553660416 | bytes 35667968 | tf_op jit(solution)/shard_map/phsir,pit->shrt/dot_general | solution.py:80
  191.3 44.2 %copy.70 = bf16[64,2,512,256]{3,2,1,0:T(8,128)(2,1)} copy(bf16[64,2,512,256]{2,3,0,1:T(8,128)(2,1)} %fusion) | data formatting | bytes 67108864 | tf_op jit(solution)/shard_map/convert_element_type | solution.py:83
  (34 shorter events, 5.9 us)
Async XLA Ops:
  26.8 7.5 %copy-start.3 = (s32[128,3]{0,1:T(4,128)S(1)}, s32[128,3]{0,1:T(4,128)}, u32[]{:S(2)}) copy-start(s32[128,3]{0,1:T(4,128)} %param.9) | copy-start | bytes 4612
  26.8 7.5 %copy-start.4 = (s32[128]{0:T(128)S(1)}, s32[128]{0:T(128)}, u32[]{:S(2)}) copy-start(s32[128]{0:T(128)} %param.8) | copy-start | bytes 1540
  26.8 7.5 %copy-start.2 = (f32[128,3]{0,1:T(4,128)S(1)}, f32[128,3]{0,1:T(4,128)}, u32[]{:S(2)}) copy-start(f32[128,3]{0,1:T(4,128)} %param.10) | copy-start | bytes 4612
  26.8 49.0 %all-to-all-start = ((bf16[16,1,2,64,512]{4,3,2,1,0:T(8,128)(2,1)}), bf16[16,1,2,64,512]{4,3,2,1,0:T(8,128)(2,1)S(1)}, u32[]{:S(2)}, u32[]{:S(2)}) async-start(bf16[16,1,2,64,512]{4,3,2,1,0:T(8,128)(2,1)} %fusion.21), calls=%async_computation | async-start | bytes 4194304 | tf_op jit(solution)/shard_map/all_to_all | solution.py:56
  75.8 1.3 copy-start
  77.1 3.9 %copy-start.1 = (bf16[16,1,2,64,512]{4,3,2,1,0:T(8,128)(2,1)S(1)}, bf16[16,1,2,64,512]{4,3,2,1,0:T(8,128)(2,1)}, u32[]{:S(2)}) copy-start(bf16[16,1,2,64,512]{4,3,2,1,0:T(8,128)(2,1)} %copy-done) | copy-start | bytes 6291460
  99.6 6.6 %collective-permute-start = (bf16[1,2,1024,512]{3,1,2,0:T(2,128)(2,1)S(1)}, bf16[1,2,1024,512]{3,1,2,0:T(2,128)(2,1)S(1)}, u32[]{:S(2)}, u32[]{:S(2)}) collective-permute-start(bf16[1,2,1024,512]{3,1,2,0:T(2,128)(2,1)S(1)} %bitcast.187), channel_id=1, source_target_pairs={{0,1},{1,0},{2,3},{3,2},{4,5},{5,4},{6,7},{7,6},{8,9},{9,8},{10,11... | collective-permute-start | bytes 6291464 | tf_op jit(solution)/shard_map/ppermute | solution.py:9
